TPU v7x, 512 devices: a whole 4x8x8 slice. The times are simulated.
512 devices in a mesh: lat: 32 (over x_hi, y, core), lon: 16 (over z, x_lo).
Axes of the slice: x: 4 (x_hi: 2, x_lo: 2; x = x_hi * 2 + x_lo), y: 8, z: 8, core: 2. Of those that a mesh axis runs over, the one named last changes fastest.
Arguments:
- features: bfloat16 [512, 1024, 128], P('lat', 'lon'), may hold values from -6 to 6
- w_first: bfloat16 [2, 1, 128, 128], replicated, may hold values from -0.375 to 0.375
- bias_first: float32 [2, 1, 128], replicated, may hold values from -3 to 3
- w_second: bfloat16 [2, 1, 128, 128], replicated, may hold values from -0.375 to 0.375
- bias_second: float32 [2, 1, 128], replicated, may hold values from -0.3 to 0.3
Outputs:
- mixed_field: bfloat16 [512, 1024, 128], P('lat', 'lon')
All inputs are finite; a program needn't handle non-finite values.
Results may differ from a plain program's by a relative error of at most 0.025.
Values may be sent and summed in bfloat16 or wider, within the bound.
A program may use at most 64 MiB of HBM per device.

v0:
```python
import math
import jax
import jax.numpy as jnp
from jax import lax
from jax.sharding import PartitionSpec as P

shrink_level = 0.01


def phase_pair(product, length, sign):
    angle_value = (product % length).astype(jnp.float32) * (sign * 2.0 * math.pi / length)
    return (jnp.cos(angle_value), jnp.sin(angle_value))


def index_outer(left_index, right_index):
    return left_index[:, None] * right_index[None, :]


def twin_dot(pattern, operand, phase_table):
    upper_part = phase_table.astype(jnp.bfloat16)
    lower_part = (phase_table - upper_part.astype(jnp.float32)).astype(jnp.bfloat16)
    return jnp.einsum(
        pattern, operand, upper_part, preferred_element_type=jnp.float32
    ) + jnp.einsum(pattern, operand, lower_part, preferred_element_type=jnp.float32)


def complex_table(pattern, real_part, imag_part, cos_table, sin_table):
    real_out = twin_dot(pattern, real_part, cos_table) - twin_dot(pattern, imag_part, sin_table)
    imag_out = twin_dot(pattern, real_part, sin_table) + twin_dot(pattern, imag_part, cos_table)
    return (real_out, imag_out)


def bit_reverse(number, levels):
    result = jnp.zeros_like(number)
    for bit_level in range(levels):
        result = result + number // 2**bit_level % 2 * 2 ** (levels - 1 - bit_level)
    return result


def local_sections(received, levels):
    full_shape = received.shape
    real_part = received.astype(jnp.float32)
    imag_part = jnp.zeros_like(real_part)
    real_half = received
    imag_half = imag_part.astype(jnp.bfloat16)
    for section_level in range(levels - 1, -1, -1):
        half_span = 2**section_level
        split_shape = (full_shape[0], full_shape[1] // (2 * half_span), 2, half_span) + full_shape[
            2:
        ]
        real_split = real_part.reshape(split_shape)
        imag_split = imag_part.reshape(split_shape)
        tw_cos, tw_sin = phase_pair(jnp.arange(half_span, dtype=jnp.int32), 2 * half_span, -1.0)
        tw_cos = tw_cos[None, None, :, None, None]
        tw_sin = tw_sin[None, None, :, None, None]
        sum_re = real_split[:, :, 0] + real_split[:, :, 1]
        sum_im = imag_split[:, :, 0] + imag_split[:, :, 1]
        diff_re = real_split[:, :, 0] - real_split[:, :, 1]
        diff_im = imag_split[:, :, 0] - imag_split[:, :, 1]
        upper_re = diff_re * tw_cos - diff_im * tw_sin
        upper_im = diff_re * tw_sin + diff_im * tw_cos
        real_half = jnp.stack([sum_re, upper_re], axis=2).reshape(full_shape).astype(jnp.bfloat16)
        imag_half = jnp.stack([sum_im, upper_im], axis=2).reshape(full_shape).astype(jnp.bfloat16)
        real_part = real_half.astype(jnp.float32)
        imag_part = imag_half.astype(jnp.float32)
    return (real_half, imag_half)


def block_product(real_part, imag_part, weights):
    real_out = jnp.einsum(
        "tnj,njk->tnk", real_part, weights[0], preferred_element_type=jnp.float32
    ) - jnp.einsum("tnj,njk->tnk", imag_part, weights[1], preferred_element_type=jnp.float32)
    imag_out = jnp.einsum(
        "tnj,njk->tnk", imag_part, weights[0], preferred_element_type=jnp.float32
    ) + jnp.einsum("tnj,njk->tnk", real_part, weights[1], preferred_element_type=jnp.float32)
    return (real_out, imag_out)


def soft_shrink(values):
    return jnp.sign(values) * jnp.maximum(jnp.abs(values) - shrink_level, 0.0)


def spectral_mix(real_part, imag_part, w_first, bias_first, w_second, bias_second):
    hid_re, hid_im = block_product(real_part, imag_part, w_first)
    act_re = jax.nn.relu(hid_re + bias_first[0]).astype(jnp.bfloat16)
    act_im = jax.nn.relu(hid_im + bias_first[1]).astype(jnp.bfloat16)
    out_re, out_im = block_product(act_re, act_im, w_second)
    return (
        soft_shrink(out_re + bias_second[0]).astype(jnp.bfloat16),
        soft_shrink(out_im + bias_second[1]).astype(jnp.bfloat16),
    )


def send_real(blocks):
    return lax.all_to_all(blocks, "lon", split_axis=1, concat_axis=1, tiled=True)


def to_columns(real_part, imag_part):
    return (
        lax.all_to_all(real_part, "lat", split_axis=1, concat_axis=0, tiled=True),
        lax.all_to_all(imag_part, "lat", split_axis=1, concat_axis=0, tiled=True),
    )


def to_rows(real_part, imag_part):
    return (
        lax.all_to_all(real_part, "lat", split_axis=0, concat_axis=1, tiled=True),
        lax.all_to_all(imag_part, "lat", split_axis=0, concat_axis=1, tiled=True),
    )


def body(features, w_first, bias_first, w_second, bias_second):
    lat_rows, lon_cells, channels = features.shape
    lon_count = lax.axis_size("lon")
    lat_count = lax.axis_size("lat")
    total_lat = lat_rows * lat_count
    total_lon = lon_cells * lon_count
    stride = lon_cells // lon_count
    keep_cells = lon_cells // 2
    norm_factor = 1.0 / math.sqrt(total_lat * total_lon)
    levels = lon_count.bit_length() - 1
    lon_place = lax.axis_index("lon")
    shard_index = jnp.arange(lon_count, dtype=jnp.int32)
    cell_index = jnp.arange(lon_cells, dtype=jnp.int32)
    keep_index = jnp.arange(keep_cells, dtype=jnp.int32)
    own_freq = bit_reverse(lon_place, levels)
    source_freq = bit_reverse(shard_index, levels)
    received = send_real(features.reshape(lat_rows, lon_count, stride, channels))
    sectioned_re, sectioned_im = local_sections(received, levels)
    cell_local = lon_place * stride + jnp.arange(stride, dtype=jnp.int32)
    rot_cos, rot_sin = phase_pair(index_outer(source_freq, cell_local), total_lon, -1.0)
    rot_cos = rot_cos[None, :, :, None]
    rot_sin = rot_sin[None, :, :, None]
    section_re = sectioned_re.astype(jnp.float32)
    section_im = sectioned_im.astype(jnp.float32)
    first_re = (section_re * rot_cos - section_im * rot_sin).astype(jnp.bfloat16)
    first_im = (section_re * rot_sin + section_im * rot_cos).astype(jnp.bfloat16)
    first_re, first_im = (
        lax.all_to_all(first_re, "lon", split_axis=1, concat_axis=1, tiled=True),
        lax.all_to_all(first_im, "lon", split_axis=1, concat_axis=1, tiled=True),
    )
    first_re = first_re.reshape(lat_rows, lon_cells, channels)
    first_im = first_im.reshape(lat_rows, lon_cells, channels)
    wave_cos, wave_sin = phase_pair(index_outer(cell_index, keep_index), lon_cells, -1.0)
    lon_re, lon_im = complex_table("rmc,mq->rqc", first_re, first_im, wave_cos, wave_sin)
    col_re, col_im = to_columns(lon_re.astype(jnp.bfloat16), lon_im.astype(jnp.bfloat16))
    row_index = jnp.arange(total_lat, dtype=jnp.int32)
    lat_cos, lat_sin = phase_pair(index_outer(row_index, row_index), total_lat, -1.0)
    spec_re, spec_im = complex_table("rqc,rl->lqc", col_re, col_im, lat_cos, lat_sin)
    spec_re = (spec_re * norm_factor).astype(jnp.bfloat16)
    spec_im = (spec_im * norm_factor).astype(jnp.bfloat16)
    mix_re, mix_im = spectral_mix(spec_re, spec_im, w_first, bias_first, w_second, bias_second)
    back_re, back_im = complex_table("lqc,lr->rqc", mix_re, mix_im, lat_cos, -lat_sin)
    back_re, back_im = to_rows(back_re.astype(jnp.bfloat16), back_im.astype(jnp.bfloat16))
    mode_weight = jnp.where((own_freq == 0) & (keep_index == 0), 1.0, 2.0).astype(jnp.float32)
    inv_cos, inv_sin = phase_pair(index_outer(keep_index, cell_index), lon_cells, 1.0)
    inv_cos = inv_cos * mode_weight[:, None]
    inv_sin = inv_sin * mode_weight[:, None]
    inv_re, inv_im = complex_table("rqc,qm->rmc", back_re, back_im, inv_cos, inv_sin)
    turn_cos, turn_sin = phase_pair(cell_index * own_freq, total_lon, 1.0)
    turn_cos = turn_cos[None, :, None]
    turn_sin = turn_sin[None, :, None]
    lon_back_re = (inv_re * turn_cos - inv_im * turn_sin).astype(jnp.bfloat16)
    lon_back_im = (inv_re * turn_sin + inv_im * turn_cos).astype(jnp.bfloat16)
    lon_back_re = lon_back_re.reshape(lat_rows, lon_count, stride, channels)
    lon_back_im = lon_back_im.reshape(lat_rows, lon_count, stride, channels)
    got_re, got_im = (
        lax.all_to_all(lon_back_re, "lon", split_axis=1, concat_axis=1, tiled=True),
        lax.all_to_all(lon_back_im, "lon", split_axis=1, concat_axis=1, tiled=True),
    )
    back_cos, back_sin = phase_pair(index_outer(source_freq, shard_index), lon_count, 1.0)
    spatial = twin_dot("rxsc,xb->rbsc", got_re, back_cos) - twin_dot(
        "rxsc,xb->rbsc", got_im, back_sin
    )
    filtered = (spatial * norm_factor).astype(jnp.bfloat16)
    filtered = send_real(filtered).reshape(lat_rows, lon_cells, channels)
    return (features.astype(jnp.float32) + filtered.astype(jnp.float32)).astype(jnp.bfloat16)


def solution(mesh):
    in_specs = (P("lat", "lon", None), P(), P(), P(), P())
    out_specs = P("lat", "lon", None)
    return jax.shard_map(body, mesh=mesh, in_specs=in_specs, out_specs=out_specs, check_vma=False)
```

profile of v0, /device:TPU:8, one launch (start us, length us, event | category | flops | bytes accessed | tf_op | source)
XLA Modules:
  0.0 246.2 jit_solution(9135461350170942632)
XLA Ops:
  1.8 11.3 %all-to-all-start = ((bf16[16,16,4,128]{3,2,0,1:T(4,128)(2,1)}), bf16[16,16,4,128]{3,2,0,1:T(4,128)(2,1)S(1)}, u32[]{:S(2)}, u32[]{:S(2)}) async-start(bf16[16,16,4,128]{3,2,0,1:T(4,128)(2,1)} %copy.37), calls=%async_computation | async-start | bytes 524288 | tf_op jit(solution)/shard_map/all_to_all | solution.py:95
  13.6 11.5 %all-to-all-done = bf16[16,16,4,128]{3,2,0,1:T(4,128)(2,1)S(1)} async-done(((bf16[16,16,4,128]{3,2,0,1:T(4,128)(2,1)}), bf16[16,16,4,128]{3,2,0,1:T(4,128)(2,1)S(1)}, u32[]{:S(2)}, u32[]{:S(2)}) %all-to-all-start) | async-done | bytes 262176 | tf_op jit(solution)/shard_map/all_to_all | solution.py:95
  34.3 9.5 %all-to-all-done.1 = bf16[16,16,4,128]{3,2,0,1:T(4,128)(2,1)S(1)} async-done(((bf16[16,16,4,128]{3,2,0,1:T(4,128)(2,1)}), bf16[16,16,4,128]{3,2,0,1:T(4,128)(2,1)S(1)}, u32[]{:S(2)}, u32[]{:S(2)}) %all-to-all-start.1) | async-done | bytes 262176 | tf_op jit(solution)/shard_map/all_to_all | solution.py:139
  48.2 9.9 %all-to-all-done.2 = bf16[16,16,4,128]{3,2,0,1:T(4,128)(2,1)S(1)} async-done(((bf16[16,16,4,128]{3,2,0,1:T(4,128)(2,1)}), bf16[16,16,4,128]{3,2,0,1:T(4,128)(2,1)S(1)}, u32[]{:S(2)}, u32[]{:S(2)}) %all-to-all-start.2) | async-done | bytes 262176 | tf_op jit(solution)/shard_map/all_to_all | solution.py:140
  59.4 9.9 %all-to-all-start.4 = ((bf16[16,32,128]{2,0,1:T(8,128)(2,1)}), bf16[16,32,128]{2,0,1:T(8,128)(2,1)S(1)}, u32[]{:S(2)}, u32[]{:S(2)}) async-start(bf16[16,32,128]{2,0,1:T(8,128)(2,1)} %copy.41), calls=%async_computation.4 | async-start | bytes 262144 | tf_op jit(solution)/shard_map/all_to_all | solution.py:101
  70.7 9.4 %all-to-all-done.4 = bf16[16,32,128]{2,0,1:T(8,128)(2,1)S(1)} async-done(((bf16[16,32,128]{2,0,1:T(8,128)(2,1)}), bf16[16,32,128]{2,0,1:T(8,128)(2,1)S(1)}, u32[]{:S(2)}, u32[]{:S(2)}) %all-to-all-start.4) | async-done | bytes 131104 | tf_op jit(solution)/shard_map/all_to_all | solution.py:101
  80.1 4.9 %all-to-all-start.3 = ((bf16[16,32,128]{2,0,1:T(8,128)(2,1)}), bf16[16,32,128]{2,0,1:T(8,128)(2,1)S(1)}, u32[]{:S(2)}, u32[]{:S(2)}) async-start(bf16[16,32,128]{2,0,1:T(8,128)(2,1)} %copy.40), calls=%async_computation.3 | async-start | bytes 262144 | tf_op jit(solution)/shard_map/all_to_all | solution.py:100
  89.7 4.7 %fusion.63 = f32[512,128]{1,0:T(8,128)S(1)} fusion(bf16[512,128]{1,0:T(8,128)(2,1)S(1)} %bitcast.283), kind=kOutput, calls=%fused_computation.94 | convolution fusion | flops 71041024 | bytes 393216 | tf_op jit(solution)/shard_map/rqc,rl->lqc/dot_general | solution.py:22
  105.3 4.7 %convolution_add_fusion.12 = f32[512,128]{1,0:T(8,128)S(1)} fusion(f32[512,128]{1,0:T(8,128)S(1)} %fusion.57, bf16[512,128]{1,0:T(8,128)(2,1)S(1)} %bitcast.284), kind=kOutput, calls=%fused_computation.26 | convolution fusion | flops 71892992 | bytes 655360 | tf_op jit(solution)/shard_map/rqc,rl->lqc/dot_general | solution.py:24
  110.1 4.8 %convolution_add_fusion.14 = f32[512,128]{1,0:T(8,128)S(1)} fusion(f32[512,128]{1,0:T(8,128)S(1)} %fusion.63, bf16[512,128]{1,0:T(8,128)(2,1)S(1)} %bitcast.285), kind=kOutput, calls=%fused_computation.28 | convolution fusion | flops 71892992 | bytes 655360 | tf_op jit(solution)/shard_map/rqc,rl->lqc/dot_general | solution.py:24
  114.8 4.8 %fusion.31 = bf16[512,128]{1,0:T(8,128)(2,1)S(1)} fusion(f32[512,128]{1,0:T(8,128)S(1)} %convolution_add_fusion.12, f32[512,128]{1,0:T(8,128)S(1)} %fusion.61, bf16[512,128]{1,0:T(8,128)(2,1)S(1)} %bitcast.288), kind=kOutput, calls=%fused_computation.56 | convolution fusion | flops 72089600 | bytes 786432 | tf_op jit(solution)/shard_map/rqc,rl->lqc/dot_general | solution.py:24
  119.8 4.7 %fusion.30 = bf16[512,128]{1,0:T(8,128)(2,1)S(1)} fusion(f32[512,128]{1,0:T(8,128)S(1)} %convolution_add_fusion.14, f32[512,128]{1,0:T(8,128)S(1)} %fusion.59, bf16[512,128]{1,0:T(8,128)(2,1)S(1)} %bitcast.289), kind=kOutput, calls=%fused_computation.55 | convolution fusion | flops 72089600 | bytes 786432 | tf_op jit(solution)/shard_map/rqc,rl->lqc/dot_general | solution.py:24
  131.0 4.8 %fusion.66 = f32[512,128]{1,0:T(8,128)S(1)} fusion(bf16[512,128]{1,0:T(8,128)(2,1)S(1)} %fusion.67), kind=kOutput, calls=%fused_computation.96 | convolution fusion | flops 71303168 | bytes 393216 | tf_op jit(solution)/shard_map/lqc,lr->rqc/dot_general | solution.py:22
  136.1 5.0 %fusion.65 = f32[512,128]{1,0:T(8,128)S(1)} fusion(bf16[512,128]{1,0:T(8,128)(2,1)S(1)} %fusion.68), kind=kOutput, calls=%fused_computation.95 | convolution fusion | flops 71303168 | bytes 393216 | tf_op jit(solution)/shard_map/lqc,lr->rqc/dot_general | solution.py:22
  145.7 4.7 %convolution_add_fusion.6 = f32[512,128]{1,0:T(8,128)S(1)} fusion(f32[512,128]{1,0:T(8,128)S(1)} %fusion.53, bf16[512,128]{1,0:T(8,128)(2,1)S(1)} %fusion.67), kind=kOutput, calls=%fused_computation.14 | convolution fusion | flops 71892992 | bytes 655360 | tf_op jit(solution)/shard_map/lqc,lr->rqc/dot_general | solution.py:24
  150.5 4.8 %fusion.37 = bf16[512,1,128]{2,0,1:T(8,128)(2,1)S(1)} fusion(f32[512,128]{1,0:T(8,128)S(1)} %convolution_add_fusion.6, f32[512,128]{1,0:T(8,128)S(1)} %fusion.65, bf16[512,128]{1,0:T(8,128)(2,1)S(1)} %fusion.68), kind=kOutput, calls=%fused_computation.62 | convolution fusion | flops 72286208 | bytes 786432 | tf_op jit(solution)/shard_map/lqc,lr->rqc/dot_general | solution.py:24
  157.3 8.4 %all-to-all-start.6 = ((bf16[32,2,1024]{2,1,0:T(2,128)(2,1)}), bf16[32,2,1024]{2,1,0:T(2,128)(2,1)S(1)}, u32[]{:S(2)}, u32[]{:S(2)}) async-start(bf16[32,2,1024]{2,1,0:T(2,128)(2,1)} %reshape.551), calls=%async_computation.6 | async-start | bytes 262144 | tf_op jit(solution)/shard_map/all_to_all | solution.py:108
  165.7 4.8 %convolution_add_fusion.8 = f32[512,128]{1,0:T(8,128)S(1)} fusion(f32[512,128]{1,0:T(8,128)S(1)} %fusion.66, bf16[512,128]{1,0:T(8,128)(2,1)S(1)} %fusion.67), kind=kOutput, calls=%fused_computation.16 | convolution fusion | flops 72155136 | bytes 655360 | tf_op jit(solution)/shard_map/lqc,lr->rqc/dot_general | solution.py:24
  170.5 4.7 %fusion.36 = bf16[512,1,128]{2,0,1:T(8,128)(2,1)S(1)} fusion(f32[512,128]{1,0:T(8,128)S(1)} %convolution_add_fusion.8, f32[512,128]{1,0:T(8,128)S(1)} %fusion.55, bf16[512,128]{1,0:T(8,128)(2,1)S(1)} %fusion.68), kind=kOutput, calls=%fused_computation.61 | convolution fusion | flops 72024064 | bytes 786432 | tf_op jit(solution)/shard_map/lqc,lr->rqc/dot_general | solution.py:24
  176.7 9.8 %all-to-all-start.5 = ((bf16[32,2,1024]{2,1,0:T(2,128)(2,1)}), bf16[32,2,1024]{2,1,0:T(2,128)(2,1)S(1)}, u32[]{:S(2)}, u32[]{:S(2)}) async-start(bf16[32,2,1024]{2,1,0:T(2,128)(2,1)} %reshape.553), calls=%async_computation.5 | async-start | bytes 262144 | tf_op jit(solution)/shard_map/all_to_all | solution.py:107
  187.3 10.0 %all-to-all-done.5 = bf16[32,2,1024]{2,1,0:T(2,128)(2,1)S(1)} async-done(((bf16[32,2,1024]{2,1,0:T(2,128)(2,1)}), bf16[32,2,1024]{2,1,0:T(2,128)(2,1)S(1)}, u32[]{:S(2)}, u32[]{:S(2)}) %all-to-all-start.5) | async-done | bytes 131104 | tf_op jit(solution)/shard_map/all_to_all | solution.py:107
  204.8 10.8 %all-to-all-done.8 = bf16[16,16,4,128]{3,2,0,1:T(4,128)(2,1)S(1)} async-done(((bf16[16,16,4,128]{3,2,0,1:T(4,128)(2,1)}), bf16[16,16,4,128]{3,2,0,1:T(4,128)(2,1)S(1)}, u32[]{:S(2)}, u32[]{:S(2)}) %all-to-all-start.8) | async-done | bytes 262176 | tf_op jit(solution)/shard_map/all_to_all | solution.py:169
  219.8 10.4 %all-to-all-done.7 = bf16[16,16,4,128]{3,2,0,1:T(4,128)(2,1)S(1)} async-done(((bf16[16,16,4,128]{3,2,0,1:T(4,128)(2,1)}), bf16[16,16,4,128]{3,2,0,1:T(4,128)(2,1)S(1)}, u32[]{:S(2)}, u32[]{:S(2)}) %all-to-all-start.7) | async-done | bytes 262176 | tf_op jit(solution)/shard_map/all_to_all | solution.py:168
  230.9 13.3 %all_to_all.96 = bf16[16,16,4,128]{3,2,0,1:T(4,128)(2,1)S(1)} all-to-all(bf16[16,16,4,128]{3,2,0,1:T(4,128)(2,1)S(1)} %copy.52), channel_id=1, replica_groups=mesh['lat'=32,'lon'=16] {'lon'}, dimensions={1} | all-to-all | bytes 524288 | tf_op jit(solution)/shard_map/all_to_all | solution.py:95
  (100 shorter events, 63.8 us)
Async XLA Ops:
  1.8 23.4 %all-to-all-start = ((bf16[16,16,4,128]{3,2,0,1:T(4,128)(2,1)}), bf16[16,16,4,128]{3,2,0,1:T(4,128)(2,1)S(1)}, u32[]{:S(2)}, u32[]{:S(2)}) async-start(bf16[16,16,4,128]{3,2,0,1:T(4,128)(2,1)} %copy.37), calls=%async_computation | async-start | bytes 524288 | tf_op jit(solution)/shard_map/all_to_all | solution.py:95
  29.4 14.4 %all-to-all-start.1 = ((bf16[16,16,4,128]{3,2,0,1:T(4,128)(2,1)}), bf16[16,16,4,128]{3,2,0,1:T(4,128)(2,1)S(1)}, u32[]{:S(2)}, u32[]{:S(2)}) async-start(bf16[16,16,4,128]{3,2,0,1:T(4,128)(2,1)} %get-tuple-element.14), calls=%async_computation.1 | async-start | bytes 524288 | tf_op jit(solution)/shard_map/all_to_all | solution.py:139
  32.9 0.7 copy-start.3
  33.6 0.7 copy-start.4
  43.8 14.3 %all-to-all-start.2 = ((bf16[16,16,4,128]{3,2,0,1:T(4,128)(2,1)}), bf16[16,16,4,128]{3,2,0,1:T(4,128)(2,1)S(1)}, u32[]{:S(2)}, u32[]{:S(2)}) async-start(bf16[16,16,4,128]{3,2,0,1:T(4,128)(2,1)} %get-tuple-element.13), calls=%async_computation.2 | async-start | bytes 524288 | tf_op jit(solution)/shard_map/all_to_all | solution.py:140
  59.4 20.7 %all-to-all-start.4 = ((bf16[16,32,128]{2,0,1:T(8,128)(2,1)}), bf16[16,32,128]{2,0,1:T(8,128)(2,1)S(1)}, u32[]{:S(2)}, u32[]{:S(2)}) async-start(bf16[16,32,128]{2,0,1:T(8,128)(2,1)} %copy.41), calls=%async_computation.4 | async-start | bytes 262144 | tf_op jit(solution)/shard_map/all_to_all | solution.py:101
  80.1 15.8 %all-to-all-start.3 = ((bf16[16,32,128]{2,0,1:T(8,128)(2,1)}), bf16[16,32,128]{2,0,1:T(8,128)(2,1)S(1)}, u32[]{:S(2)}, u32[]{:S(2)}) async-start(bf16[16,32,128]{2,0,1:T(8,128)(2,1)} %copy.40), calls=%async_computation.3 | async-start | bytes 262144 | tf_op jit(solution)/shard_map/all_to_all | solution.py:100
  114.8 4.8 %copy-start.1 = (bf16[2,1,128,128]{3,2,1,0:T(8,128)(2,1)S(1)}, bf16[2,1,128,128]{3,2,1,0:T(8,128)(2,1)}, u32[]{:S(2)}) copy-start(bf16[2,1,128,128]{3,2,1,0:T(8,128)(2,1)} %param.6) | copy-start | bytes 196612
  124.7 0.8 copy-start.2
  157.3 19.4 %all-to-all-start.6 = ((bf16[32,2,1024]{2,1,0:T(2,128)(2,1)}), bf16[32,2,1024]{2,1,0:T(2,128)(2,1)S(1)}, u32[]{:S(2)}, u32[]{:S(2)}) async-start(bf16[32,2,1024]{2,1,0:T(2,128)(2,1)} %reshape.551), calls=%async_computation.6 | async-start | bytes 262144 | tf_op jit(solution)/shard_map/all_to_all | solution.py:108
  176.7 20.7 %all-to-all-start.5 = ((bf16[32,2,1024]{2,1,0:T(2,128)(2,1)}), bf16[32,2,1024]{2,1,0:T(2,128)(2,1)S(1)}, u32[]{:S(2)}, u32[]{:S(2)}) async-start(bf16[32,2,1024]{2,1,0:T(2,128)(2,1)} %reshape.553), calls=%async_computation.5 | async-start | bytes 262144 | tf_op jit(solution)/shard_map/all_to_all | solution.py:107
  200.5 15.1 %all-to-all-start.8 = ((bf16[16,16,4,128]{3,2,0,1:T(4,128)(2,1)}), bf16[16,16,4,128]{3,2,0,1:T(4,128)(2,1)S(1)}, u32[]{:S(2)}, u32[]{:S(2)}) async-start(bf16[16,16,4,128]{3,2,0,1:T(4,128)(2,1)} %copy.49), calls=%async_computation.8 | async-start | bytes 524288 | tf_op jit(solution)/shard_map/all_to_all | solution.py:169
  215.6 14.6 %all-to-all-start.7 = ((bf16[16,16,4,128]{3,2,0,1:T(4,128)(2,1)}), bf16[16,16,4,128]{3,2,0,1:T(4,128)(2,1)S(1)}, u32[]{:S(2)}, u32[]{:S(2)}) async-start(bf16[16,16,4,128]{3,2,0,1:T(4,128)(2,1)} %copy.46), calls=%async_computation.7 | async-start | bytes 524288 | tf_op jit(solution)/shard_map/all_to_all | solution.py:168
  244.3 1.0 copy-start
where the time goes:
time: 247 us; the launch traced here: 246 us
  matrix products  83.4 us (34%)
  waiting for transfers between devices  73 us (30%)
  starting transfers between devices  58.5 us (24%)
  blocking collectives  13.3 us (5%)
  local copies, waits for them, and re-layouts  11.2 us (5%)
  other arithmetic  6.01 us (2%)
    dot_general x18, matrix products, twin_dot(): jnp.einsum(pattern, operand, lower_part, preferred_element_type=jnp.float32)  41.1 us
    dot_general x18, matrix products, twin_dot(): jnp.einsum(pattern, operand, upper_part, preferred_element_type=jnp.float32)  40.8 us
    all_to_all x1, blocking collectives, send_real(): lax.all_to_all(blocks, 'lon', split_axis=1, concat_axis=1, tiled=True)  13.3 us
    all_to_all x1, waiting for transfers between devices, send_real(): lax.all_to_all(blocks, 'lon', split_axis=1, concat_axis=1, tiled=True)  11.5 us
    all_to_all x1, starting transfers between devices, send_real(): lax.all_to_all(blocks, 'lon', split_axis=1, concat_axis=1, tiled=True)  11.3 us
    all_to_all x1, waiting for transfers between devices, body(): lax.all_to_all(lon_back_im, 'lon', split_axis=1, concat_axis=1, tiled=True)  10.8 us
    all_to_all x1, waiting for transfers between devices, body(): lax.all_to_all(lon_back_re, 'lon', split_axis=1, concat_axis=1, tiled=True)  10.4 us
    all_to_all x1, waiting for transfers between devices, to_rows(): lax.all_to_all(real_part, 'lat', split_axis=0, concat_axis=1, tiled=True)  10 us
  transfers between devices with their start and end apart: 9, of which 8 were waited for; matrix products, arithmetic and copies ran while one was open for 10% of the time, Pallas kernels for 0%

commit v1 on v0

--- a/solution.py
+++ b/solution.py
@@ -136,7 +136,12 @@
     first_re = (section_re * rot_cos - section_im * rot_sin).astype(jnp.bfloat16)
     first_im = (section_re * rot_sin + section_im * rot_cos).astype(jnp.bfloat16)
     first_re, first_im = (
-        lax.all_to_all(first_re, "lon", split_axis=1, concat_axis=1, tiled=True),
+        jnp.concatenate(
+            lax.all_to_all(
+                jnp.stack(jnp.split(first_re, lax.axis_size("lon"), axis=1)), "lon", 0, 0
+            ),
+            axis=1,
+        ),
         lax.all_to_all(first_im, "lon", split_axis=1, concat_axis=1, tiled=True),
     )
     first_re = first_re.reshape(lat_rows, lon_cells, channels)

time: 247 us -> 257 us (1.040)
  the two profiles are of different devices: /device:TPU:8 before, /device:TPU:16 now
where the time goes in v1:
time: 257 us; the launch traced here: 256 us
  matrix products  83.4 us (32%)
  waiting for transfers between devices  70 us (27%)
  starting transfers between devices  61.3 us (24%)
  local copies, waits for them, and re-layouts  20.9 us (8%)
  blocking collectives  13.3 us (5%)
  other arithmetic  5.93 us (2%)
    dot_general x18, matrix products, twin_dot(): jnp.einsum(pattern, operand, lower_part, preferred_element_type=jnp.float32)  41.1 us
    dot_general x18, matrix products, twin_dot(): jnp.einsum(pattern, operand, upper_part, preferred_element_type=jnp.float32)  40.8 us
    unnamed x31, local copies, waits for them, and re-layouts  13.6 us
    all_to_all x1, blocking collectives, send_real(): lax.all_to_all(blocks, 'lon', split_axis=1, concat_axis=1, tiled=True)  13.3 us
    all_to_all x1, waiting for transfers between devices, body(): lax.all_to_all(lon_back_im, 'lon', split_axis=1, concat_axis=1, tiled=True)  12.2 us
    all_to_all x1, waiting for transfers between devices, send_real(): lax.all_to_all(blocks, 'lon', split_axis=1, concat_axis=1, tiled=True)  11.5 us
    all_to_all x1, starting transfers between devices, send_real(): lax.all_to_all(blocks, 'lon', split_axis=1, concat_axis=1, tiled=True)  11.3 us
    all_to_all x1, waiting for transfers between devices, body(): lax.all_to_all(lon_back_re, 'lon', split_axis=1, concat_axis=1, tiled=True)  10.3 us
  transfers between devices with their start and end apart: 9, of which 7 were waited for; matrix products, arithmetic and copies ran while one was open for 10% of the time, Pallas kernels for 0%

profile of v1, /device:TPU:16, one launch (start us, length us, event | category | flops | bytes accessed | tf_op | source)
XLA Modules:
  0.0 255.6 jit_solution(12315452039150286028)
XLA Ops:
  1.8 11.3 %all-to-all-start = ((bf16[16,16,4,128]{3,2,0,1:T(4,128)(2,1)}), bf16[16,16,4,128]{3,2,0,1:T(4,128)(2,1)S(1)}, u32[]{:S(2)}, u32[]{:S(2)}) async-start(bf16[16,16,4,128]{3,2,0,1:T(4,128)(2,1)} %copy.73), calls=%async_computation | async-start | bytes 524288 | tf_op jit(solution)/shard_map/all_to_all | solution.py:95
  13.6 11.5 %all-to-all-done = bf16[16,16,4,128]{3,2,0,1:T(4,128)(2,1)S(1)} async-done(((bf16[16,16,4,128]{3,2,0,1:T(4,128)(2,1)}), bf16[16,16,4,128]{3,2,0,1:T(4,128)(2,1)S(1)}, u32[]{:S(2)}, u32[]{:S(2)}) %all-to-all-start) | async-done | bytes 262176 | tf_op jit(solution)/shard_map/all_to_all | solution.py:95
  43.9 9.5 %all-to-all-done.1 = bf16[16,16,1,4,128]{4,3,1,2,0:T(4,128)(2,1)S(1)} async-done(((bf16[16,16,1,4,128]{4,3,1,2,0:T(4,128)(2,1)}), bf16[16,16,1,4,128]{4,3,1,2,0:T(4,128)(2,1)S(1)}, u32[]{:S(2)}, u32[]{:S(2)}) %all-to-all-start.1) | async-done | bytes 262176 | tf_op jit(solution)/shard_map/all_to_all | solution.py:140
  57.8 9.9 %all-to-all-done.2 = bf16[16,16,4,128]{3,2,0,1:T(4,128)(2,1)S(1)} async-done(((bf16[16,16,4,128]{3,2,0,1:T(4,128)(2,1)}), bf16[16,16,4,128]{3,2,0,1:T(4,128)(2,1)S(1)}, u32[]{:S(2)}, u32[]{:S(2)}) %all-to-all-start.2) | async-done | bytes 262176 | tf_op jit(solution)/shard_map/all_to_all | solution.py:145
  69.0 9.8 %all-to-all-start.4 = ((bf16[16,32,128]{2,0,1:T(8,128)(2,1)}), bf16[16,32,128]{2,0,1:T(8,128)(2,1)S(1)}, u32[]{:S(2)}, u32[]{:S(2)}) async-start(bf16[16,32,128]{2,0,1:T(8,128)(2,1)} %copy.77), calls=%async_computation.4 | async-start | bytes 262144 | tf_op jit(solution)/shard_map/all_to_all | solution.py:101
  80.2 7.9 %all-to-all-done.4 = bf16[16,32,128]{2,0,1:T(8,128)(2,1)S(1)} async-done(((bf16[16,32,128]{2,0,1:T(8,128)(2,1)}), bf16[16,32,128]{2,0,1:T(8,128)(2,1)S(1)}, u32[]{:S(2)}, u32[]{:S(2)}) %all-to-all-start.4) | async-done | bytes 131104 | tf_op jit(solution)/shard_map/all_to_all | solution.py:101
  88.1 6.4 %all-to-all-start.3 = ((bf16[16,32,128]{2,0,1:T(8,128)(2,1)}), bf16[16,32,128]{2,0,1:T(8,128)(2,1)S(1)}, u32[]{:S(2)}, u32[]{:S(2)}) async-start(bf16[16,32,128]{2,0,1:T(8,128)(2,1)} %copy.76), calls=%async_computation.3 | async-start | bytes 262144 | tf_op jit(solution)/shard_map/all_to_all | solution.py:100
  99.2 4.7 %fusion.63 = f32[512,128]{1,0:T(8,128)S(1)} fusion(bf16[512,128]{1,0:T(8,128)(2,1)S(1)} %bitcast.349), kind=kOutput, calls=%fused_computation.94 | convolution fusion | flops 71041024 | bytes 393216 | tf_op jit(solution)/shard_map/rqc,rl->lqc/dot_general | solution.py:22
  113.3 4.7 %convolution_add_fusion.12 = f32[512,128]{1,0:T(8,128)S(1)} fusion(f32[512,128]{1,0:T(8,128)S(1)} %fusion.57, bf16[512,128]{1,0:T(8,128)(2,1)S(1)} %bitcast.350), kind=kOutput, calls=%fused_computation.26 | convolution fusion | flops 71892992 | bytes 655360 | tf_op jit(solution)/shard_map/rqc,rl->lqc/dot_general | solution.py:24
  118.1 4.8 %convolution_add_fusion.14 = f32[512,128]{1,0:T(8,128)S(1)} fusion(f32[512,128]{1,0:T(8,128)S(1)} %fusion.63, bf16[512,128]{1,0:T(8,128)(2,1)S(1)} %bitcast.351), kind=kOutput, calls=%fused_computation.28 | convolution fusion | flops 71892992 | bytes 655360 | tf_op jit(solution)/shard_map/rqc,rl->lqc/dot_general | solution.py:24
  122.9 4.8 %fusion.31 = bf16[512,128]{1,0:T(8,128)(2,1)S(1)} fusion(f32[512,128]{1,0:T(8,128)S(1)} %convolution_add_fusion.12, f32[512,128]{1,0:T(8,128)S(1)} %fusion.61, bf16[512,128]{1,0:T(8,128)(2,1)S(1)} %bitcast.354), kind=kOutput, calls=%fused_computation.56 | convolution fusion | flops 72089600 | bytes 786432 | tf_op jit(solution)/shard_map/rqc,rl->lqc/dot_general | solution.py:24
  127.8 4.7 %fusion.30 = bf16[512,128]{1,0:T(8,128)(2,1)S(1)} fusion(f32[512,128]{1,0:T(8,128)S(1)} %convolution_add_fusion.14, f32[512,128]{1,0:T(8,128)S(1)} %fusion.59, bf16[512,128]{1,0:T(8,128)(2,1)S(1)} %bitcast.355), kind=kOutput, calls=%fused_computation.55 | convolution fusion | flops 72089600 | bytes 786432 | tf_op jit(solution)/shard_map/rqc,rl->lqc/dot_general | solution.py:24
  139.1 4.8 %fusion.66 = f32[512,128]{1,0:T(8,128)S(1)} fusion(bf16[512,128]{1,0:T(8,128)(2,1)S(1)} %fusion.67), kind=kOutput, calls=%fused_computation.96 | convolution fusion | flops 71303168 | bytes 393216 | tf_op jit(solution)/shard_map/lqc,lr->rqc/dot_general | solution.py:22
  144.1 5.0 %fusion.65 = f32[512,128]{1,0:T(8,128)S(1)} fusion(bf16[512,128]{1,0:T(8,128)(2,1)S(1)} %fusion.68), kind=kOutput, calls=%fused_computation.95 | convolution fusion | flops 71303168 | bytes 393216 | tf_op jit(solution)/shard_map/lqc,lr->rqc/dot_general | solution.py:22
  153.8 4.7 %convolution_add_fusion.6 = f32[512,128]{1,0:T(8,128)S(1)} fusion(f32[512,128]{1,0:T(8,128)S(1)} %fusion.53, bf16[512,128]{1,0:T(8,128)(2,1)S(1)} %fusion.67), kind=kOutput, calls=%fused_computation.14 | convolution fusion | flops 71892992 | bytes 655360 | tf_op jit(solution)/shard_map/lqc,lr->rqc/dot_general | solution.py:24
  158.5 4.8 %fusion.37 = bf16[512,1,128]{2,0,1:T(8,128)(2,1)S(1)} fusion(f32[512,128]{1,0:T(8,128)S(1)} %convolution_add_fusion.6, f32[512,128]{1,0:T(8,128)S(1)} %fusion.65, bf16[512,128]{1,0:T(8,128)(2,1)S(1)} %fusion.68), kind=kOutput, calls=%fused_computation.62 | convolution fusion | flops 72286208 | bytes 786432 | tf_op jit(solution)/shard_map/lqc,lr->rqc/dot_general | solution.py:24
  165.3 9.9 %all-to-all-start.6 = ((bf16[32,2,1024]{2,1,0:T(2,128)(2,1)}), bf16[32,2,1024]{2,1,0:T(2,128)(2,1)S(1)}, u32[]{:S(2)}, u32[]{:S(2)}) async-start(bf16[32,2,1024]{2,1,0:T(2,128)(2,1)} %reshape.551), calls=%async_computation.6 | async-start | bytes 262144 | tf_op jit(solution)/shard_map/all_to_all | solution.py:108
  175.2 4.8 %convolution_add_fusion.8 = f32[512,128]{1,0:T(8,128)S(1)} fusion(f32[512,128]{1,0:T(8,128)S(1)} %fusion.66, bf16[512,128]{1,0:T(8,128)(2,1)S(1)} %fusion.67), kind=kOutput, calls=%fused_computation.16 | convolution fusion | flops 72155136 | bytes 655360 | tf_op jit(solution)/shard_map/lqc,lr->rqc/dot_general | solution.py:24
  180.0 4.7 %fusion.36 = bf16[512,1,128]{2,0,1:T(8,128)(2,1)S(1)} fusion(f32[512,128]{1,0:T(8,128)S(1)} %convolution_add_fusion.8, f32[512,128]{1,0:T(8,128)S(1)} %fusion.55, bf16[512,128]{1,0:T(8,128)(2,1)S(1)} %fusion.68), kind=kOutput, calls=%fused_computation.61 | convolution fusion | flops 72024064 | bytes 786432 | tf_op jit(solution)/shard_map/lqc,lr->rqc/dot_general | solution.py:24
  186.2 9.8 %all-to-all-start.5 = ((bf16[32,2,1024]{2,1,0:T(2,128)(2,1)}), bf16[32,2,1024]{2,1,0:T(2,128)(2,1)S(1)}, u32[]{:S(2)}, u32[]{:S(2)}) async-start(bf16[32,2,1024]{2,1,0:T(2,128)(2,1)} %reshape.553), calls=%async_computation.5 | async-start | bytes 262144 | tf_op jit(solution)/shard_map/all_to_all | solution.py:107
  196.8 8.6 %all-to-all-done.5 = bf16[32,2,1024]{2,1,0:T(2,128)(2,1)S(1)} async-done(((bf16[32,2,1024]{2,1,0:T(2,128)(2,1)}), bf16[32,2,1024]{2,1,0:T(2,128)(2,1)S(1)}, u32[]{:S(2)}, u32[]{:S(2)}) %all-to-all-start.5) | async-done | bytes 131104 | tf_op jit(solution)/shard_map/all_to_all | solution.py:107
  212.9 12.2 %all-to-all-done.8 = bf16[16,16,4,128]{3,2,0,1:T(4,128)(2,1)S(1)} async-done(((bf16[16,16,4,128]{3,2,0,1:T(4,128)(2,1)}), bf16[16,16,4,128]{3,2,0,1:T(4,128)(2,1)S(1)}, u32[]{:S(2)}, u32[]{:S(2)}) %all-to-all-start.8) | async-done | bytes 262176 | tf_op jit(solution)/shard_map/all_to_all | solution.py:174
  229.3 10.3 %all-to-all-done.7 = bf16[16,16,4,128]{3,2,0,1:T(4,128)(2,1)S(1)} async-done(((bf16[16,16,4,128]{3,2,0,1:T(4,128)(2,1)}), bf16[16,16,4,128]{3,2,0,1:T(4,128)(2,1)S(1)}, u32[]{:S(2)}, u32[]{:S(2)}) %all-to-all-start.7) | async-done | bytes 262176 | tf_op jit(solution)/shard_map/all_to_all | solution.py:173
  240.4 13.3 %all_to_all.96 = bf16[16,16,4,128]{3,2,0,1:T(4,128)(2,1)S(1)} all-to-all(bf16[16,16,4,128]{3,2,0,1:T(4,128)(2,1)S(1)} %copy.88), channel_id=1, replica_groups=mesh['lat'=32,'lon'=16] {'lon'}, dimensions={1} | all-to-all | bytes 524288 | tf_op jit(solution)/shard_map/all_to_all | solution.py:95
  (116 shorter events, 71.9 us)
Async XLA Ops:
  1.8 23.4 %all-to-all-start = ((bf16[16,16,4,128]{3,2,0,1:T(4,128)(2,1)}), bf16[16,16,4,128]{3,2,0,1:T(4,128)(2,1)S(1)}, u32[]{:S(2)}, u32[]{:S(2)}) async-start(bf16[16,16,4,128]{3,2,0,1:T(4,128)(2,1)} %copy.73), calls=%async_computation | async-start | bytes 524288 | tf_op jit(solution)/shard_map/all_to_all | solution.py:95
  39.0 14.4 %all-to-all-start.1 = ((bf16[16,16,1,4,128]{4,3,1,2,0:T(4,128)(2,1)}), bf16[16,16,1,4,128]{4,3,1,2,0:T(4,128)(2,1)S(1)}, u32[]{:S(2)}, u32[]{:S(2)}) async-start(bf16[16,16,1,4,128]{4,3,1,2,0:T(4,128)(2,1)} %constant_dynamic-update-slice_fusion), calls=%async_computation.1 | async-start | bytes 524288 | tf_op jit(solution)/shard_map/all_to_all | solution.py:140
  42.5 0.7 copy-start.3
  43.2 0.7 copy-start.4
  53.4 14.3 %all-to-all-start.2 = ((bf16[16,16,4,128]{3,2,0,1:T(4,128)(2,1)}), bf16[16,16,4,128]{3,2,0,1:T(4,128)(2,1)S(1)}, u32[]{:S(2)}, u32[]{:S(2)}) async-start(bf16[16,16,4,128]{3,2,0,1:T(4,128)(2,1)} %get-tuple-element.13), calls=%async_computation.2 | async-start | bytes 524288 | tf_op jit(solution)/shard_map/all_to_all | solution.py:145
  69.0 19.1 %all-to-all-start.4 = ((bf16[16,32,128]{2,0,1:T(8,128)(2,1)}), bf16[16,32,128]{2,0,1:T(8,128)(2,1)S(1)}, u32[]{:S(2)}, u32[]{:S(2)}) async-start(bf16[16,32,128]{2,0,1:T(8,128)(2,1)} %copy.77), calls=%async_computation.4 | async-start | bytes 262144 | tf_op jit(solution)/shard_map/all_to_all | solution.py:101
  88.1 15.8 %all-to-all-start.3 = ((bf16[16,32,128]{2,0,1:T(8,128)(2,1)}), bf16[16,32,128]{2,0,1:T(8,128)(2,1)S(1)}, u32[]{:S(2)}, u32[]{:S(2)}) async-start(bf16[16,32,128]{2,0,1:T(8,128)(2,1)} %copy.76), calls=%async_computation.3 | async-start | bytes 262144 | tf_op jit(solution)/shard_map/all_to_all | solution.py:100
  122.8 4.8 %copy-start.1 = (bf16[2,1,128,128]{3,2,1,0:T(8,128)(2,1)S(1)}, bf16[2,1,128,128]{3,2,1,0:T(8,128)(2,1)}, u32[]{:S(2)}) copy-start(bf16[2,1,128,128]{3,2,1,0:T(8,128)(2,1)} %param.6) | copy-start | bytes 196612
  132.7 0.8 copy-start.2
  165.3 20.9 %all-to-all-start.6 = ((bf16[32,2,1024]{2,1,0:T(2,128)(2,1)}), bf16[32,2,1024]{2,1,0:T(2,128)(2,1)S(1)}, u32[]{:S(2)}, u32[]{:S(2)}) async-start(bf16[32,2,1024]{2,1,0:T(2,128)(2,1)} %reshape.551), calls=%async_computation.6 | async-start | bytes 262144 | tf_op jit(solution)/shard_map/all_to_all | solution.py:108
  186.2 19.2 %all-to-all-start.5 = ((bf16[32,2,1024]{2,1,0:T(2,128)(2,1)}), bf16[32,2,1024]{2,1,0:T(2,128)(2,1)S(1)}, u32[]{:S(2)}, u32[]{:S(2)}) async-start(bf16[32,2,1024]{2,1,0:T(2,128)(2,1)} %reshape.553), calls=%async_computation.5 | async-start | bytes 262144 | tf_op jit(solution)/shard_map/all_to_all | solution.py:107
  208.5 16.6 %all-to-all-start.8 = ((bf16[16,16,4,128]{3,2,0,1:T(4,128)(2,1)}), bf16[16,16,4,128]{3,2,0,1:T(4,128)(2,1)S(1)}, u32[]{:S(2)}, u32[]{:S(2)}) async-start(bf16[16,16,4,128]{3,2,0,1:T(4,128)(2,1)} %copy.85), calls=%async_computation.8 | async-start | bytes 524288 | tf_op jit(solution)/shard_map/all_to_all | solution.py:174
  225.1 14.5 %all-to-all-start.7 = ((bf16[16,16,4,128]{3,2,0,1:T(4,128)(2,1)}), bf16[16,16,4,128]{3,2,0,1:T(4,128)(2,1)S(1)}, u32[]{:S(2)}, u32[]{:S(2)}) async-start(bf16[16,16,4,128]{3,2,0,1:T(4,128)(2,1)} %copy.82), calls=%async_computation.7 | async-start | bytes 524288 | tf_op jit(solution)/shard_map/all_to_all | solution.py:173
  253.7 1.0 copy-start
